TPU v7x, 256 devices: a whole 4x4x8 slice. The times are simulated.
256 devices in a mesh: gx: 8 (over z), gy: 32 (over x, y, core).
Axes of the slice: x: 4, y: 4, z: 8, core: 2. Of those that a mesh axis runs over, the one named last changes fastest.
Arguments:
- permeability: float32 [3, 256, 65536], P(None, 'gx', 'gy'), may hold values from 0.03 to 1000, as said below
Outputs:
- fine_pressure: float32 [256, 65536], P('gx', 'gy')
- twin_pressure: float32 [128, 16384], P('gx', 'gy')
Inputs may be any that keep to these rules, and one draw needn't show every extreme that they name: `permeability`: positive conductivities; entry 0, 1, 2 of the first dimension is the conductivity along the grid's first, second, third dimension.
All inputs are finite; a program needn't handle non-finite values.
Results may differ from a plain program's by a relative error of at most 0.0003.
Values sent between devices are 32-bit elements; how exact they have to be, the bound alone decides.
A program may use at most 192 MiB of HBM per device.

v0:
```python
import jax
import jax.numpy as jnp
from jax import lax
from jax.sharding import PartitionSpec as P

EL = 32
ELZ = 16
MX = 4
MZ = 2
EZ = 2
PATCH_ITERS = 3
COARSE_ITERS = 2


def shifted(shard, axis, by):
    count = lax.axis_size(axis)
    return lax.ppermute(shard, axis, [(i, (i + by) % count) for i in range(count)])


def padded_2(cells, sides, width):
    for axis, dim in sides:
        count = lax.axis_size(axis)
        head = lax.slice_in_dim(cells, 0, width, axis=dim)
        tail = lax.slice_in_dim(cells, cells.shape[dim] - width, cells.shape[dim], axis=dim)
        cells = jnp.concatenate(
            [
                lax.ppermute(tail, axis, [(i, (i + 1) % count) for i in range(count)]),
                cells,
                lax.ppermute(head, axis, [((i + 1) % count, i) for i in range(count)]),
            ],
            axis=dim,
        )
    return cells


def harmonic(first, second, spacing):
    return spacing * 2.0 * first * second / (first + second)


def face_weights(conduct, width, spacing):
    weight_rows = harmonic(conduct[0][..., :-width], conduct[0][..., width:], spacing)
    weight_cols = harmonic(conduct[1][..., :-1], conduct[1][..., 1:], spacing)
    column = jnp.arange(weight_cols.shape[-1], dtype=jnp.int32) % width
    weight_cols = jnp.where(column == width - 1, jnp.zeros_like(weight_cols), weight_cols)
    weight_depth = harmonic(conduct[2][:, :-1], conduct[2][:, 1:], spacing)
    return (weight_rows, weight_cols, weight_depth)


def apply_operator(field, weights, width):
    weight_rows, weight_cols, weight_depth = weights
    flux = weight_rows * (field[..., :-width] - field[..., width:])
    result = jnp.pad(flux, ((0, 0), (0, 0), (0, 0), (0, width))) - jnp.pad(
        flux, ((0, 0), (0, 0), (0, 0), (width, 0))
    )
    flux = weight_cols * (field[..., :-1] - field[..., 1:])
    result = (
        result
        + jnp.pad(flux, ((0, 0), (0, 0), (0, 0), (0, 1)))
        - jnp.pad(flux, ((0, 0), (0, 0), (0, 0), (1, 0)))
    )
    flux = weight_depth * (field[:, :, :-1] - field[:, :, 1:])
    result = (
        result
        + jnp.pad(flux, ((0, 0), (0, 0), (0, 1), (0, 0)))
        - jnp.pad(flux, ((0, 0), (0, 0), (1, 0), (0, 0)))
    )
    return result


def interior_mask(depth, rows, width):
    level = jnp.arange(depth, dtype=jnp.int32)[:, None]
    cell = jnp.arange(rows * width, dtype=jnp.int32)[None, :]
    row_index = cell // width
    line_index = cell % width
    inside = (
        (level > 0)
        & (level < depth - 1)
        & (row_index > 0)
        & (row_index < rows - 1)
        & (line_index > 0)
        & (line_index < width - 1)
    )
    return inside.astype(jnp.float32)


def shape_functions(depth, rows, width, edge, edge_depth, margin, margin_depth):
    cell = jnp.arange(rows * width, dtype=jnp.int32)
    place_rows = ((cell // width).astype(jnp.float32) - margin + 0.5) / edge
    place_cols = ((cell % width).astype(jnp.float32) - margin + 0.5) / edge
    place_depth = (
        jnp.arange(depth, dtype=jnp.int32).astype(jnp.float32) - margin_depth + 0.5
    ) / edge_depth
    factors = []
    for basis in range(8):
        along_rows = place_rows if basis // 4 else 1.0 - place_rows
        along_cols = place_cols if basis // 2 % 2 else 1.0 - place_cols
        along_depth = place_depth if basis % 2 else 1.0 - place_depth
        factors.append(along_depth[:, None] * (along_rows * along_cols)[None, :])
    return jnp.stack(factors)[:, None]


def patch_fields(block, edge_depth, margin_depth):
    depth = edge_depth + 2 * margin_depth
    count = (block.shape[3] - 2 * margin_depth) // edge_depth
    pieces = [
        block[:, :, :, index * edge_depth : index * edge_depth + depth] for index in range(count)
    ]
    stacked = jnp.stack(pieces, axis=1)
    return jnp.transpose(stacked, (0, 1, 4, 2, 3)).reshape(
        3, count, depth, block.shape[1] * block.shape[2]
    )


def solve_column(block, edge, edge_depth, margin, margin_depth, spacing):
    rows = block.shape[1]
    width = block.shape[2]
    depth = edge_depth + 2 * margin_depth
    conduct = patch_fields(block, edge_depth, margin_depth)
    count = conduct.shape[1]
    weights = face_weights(conduct, width, spacing)
    inside = interior_mask(depth, rows, width)
    start = shape_functions(depth, rows, width, edge, edge_depth, margin, margin_depth)
    residual = -inside * apply_operator(start, weights, width)
    direction = residual
    norm_now = jnp.sum(residual * residual, axis=(2, 3), keepdims=True)
    update = jnp.zeros_like(residual)
    for step in range(PATCH_ITERS):
        image = inside * apply_operator(direction, weights, width)
        alpha = norm_now / jnp.sum(direction * image, axis=(2, 3), keepdims=True)
        update = update + alpha * direction
        residual = residual - alpha * image
        norm_next = jnp.sum(residual * residual, axis=(2, 3), keepdims=True)
        direction = residual + norm_next / norm_now * direction
        norm_now = norm_next
    solution = start + update
    local = solution.reshape(8, count, depth, rows, width)[
        :,
        :,
        margin_depth : margin_depth + edge_depth,
        margin : margin + edge,
        margin : margin + edge,
    ]
    local = local.reshape(8, count, edge_depth, edge * edge)
    element_conduct = conduct.reshape(3, count, depth, rows, width)[
        :,
        :,
        margin_depth : margin_depth + edge_depth,
        margin : margin + edge,
        margin : margin + edge,
    ]
    element_conduct = element_conduct.reshape(3, count, edge_depth, edge * edge)
    inner_rows, inner_cols, inner_depth = face_weights(element_conduct, edge, spacing)
    jump = local[..., :-edge] - local[..., edge:]
    stiffness = jnp.einsum(
        "aezn,bezn->eab", jump * inner_rows, jump, precision=lax.Precision.HIGHEST
    )
    jump = local[..., :-1] - local[..., 1:]
    stiffness = stiffness + jnp.einsum(
        "aezn,bezn->eab", jump * inner_cols, jump, precision=lax.Precision.HIGHEST
    )
    jump = local[:, :, :-1] - local[:, :, 1:]
    stiffness = stiffness + jnp.einsum(
        "aezn,bezn->eab", jump * inner_depth, jump, precision=lax.Precision.HIGHEST
    )
    return (local, stiffness)


def coarsen(block):
    comps, rows, width, depth = block.shape
    grouped = block.reshape(comps, rows // 2, 2, width // 2, 2, depth // 2, 2)
    return 0.125 * jnp.sum(grouped, axis=(2, 4, 6))


def corner_stack(corner_first, corner_rows, corner_cols, corner_both, count):
    table = [[corner_first, corner_cols], [corner_rows, corner_both]]
    values = []
    for basis in range(8):
        lift = basis % 2
        values.append(table[basis // 4][basis // 2 % 2][..., lift : lift + count])
    return jnp.stack(values, axis=-1)


def spread(values):
    parts = [[None, None], [None, None]]
    for basis in range(8):
        lift = basis % 2
        widths = [(0, 0)] * (values.ndim - 2) + [(lift, 1 - lift)]
        padded = jnp.pad(values[..., basis], widths)
        first = basis // 4
        second = basis // 2 % 2
        if parts[first][second] is None:
            parts[first][second] = padded
        else:
            parts[first][second] = parts[first][second] + padded
    return parts


def pressure_tile(local, weights, edge):
    combined = jnp.sum(jnp.transpose(weights)[:, :, None, None] * local, axis=0)
    count = combined.shape[0]
    depth = combined.shape[1]
    return jnp.transpose(combined.reshape(count, depth, edge, edge), (2, 3, 0, 1)).reshape(
        edge, edge, count * depth
    )


def neighbours(nodes):
    next_rows = shifted(nodes, "gx", -1)
    fetched = shifted(jnp.stack([nodes[:, 0], next_rows[:, 0]]), "gy", -1)
    next_cols = jnp.concatenate([nodes[:, 1:], fetched[0][:, None]], axis=1)
    next_both = jnp.concatenate([next_rows[:, 1:], fetched[1][:, None]], axis=1)
    return (next_rows, next_cols, next_both)


def local_operator(stiffness, nodes, count):
    next_rows, next_cols, next_both = neighbours(nodes)
    element = corner_stack(nodes, next_rows, next_cols, next_both, count)
    local = jnp.einsum("lckab,lckb->lcka", stiffness, element, precision=lax.Precision.HIGHEST)
    parts = spread(local)
    col_part = parts[0][1]
    both_part = parts[1][1]
    returned = shifted(jnp.stack([col_part[:, -1], both_part[:, -1]]), "gy", 1)
    moved_cols = jnp.concatenate([returned[0][:, None], col_part[:, :-1]], axis=1)
    moved_both = jnp.concatenate([returned[1][:, None], both_part[:, :-1]], axis=1)
    across = shifted(parts[1][0] + moved_both, "gx", 1)
    return parts[0][0] + moved_cols + across


def squares(residual):
    return lax.psum(jnp.sum(residual * residual, axis=(1, 2), keepdims=True), ("gx", "gy"))


def spread_solve(stiffness, columns, count):
    level = jnp.arange(count + 1, dtype=jnp.int32)
    inside = ((level > 0) & (level < count)).astype(jnp.float32)
    boundary = jnp.broadcast_to((level == 0).astype(jnp.float32), (2, columns, count + 1))
    source = -inside * local_operator(stiffness, boundary, count)
    update = jnp.zeros_like(source)
    residual = source
    direction = source
    norm_now = squares(residual)
    for step in range(COARSE_ITERS):
        image = inside * local_operator(stiffness, direction, count)
        alpha = norm_now / lax.psum(
            jnp.sum(direction * image, axis=(1, 2), keepdims=True), ("gx", "gy")
        )
        update = update + alpha * direction
        residual = residual - alpha * image
        norm_next = squares(residual)
        direction = residual + norm_next / norm_now * direction
        norm_now = norm_next
    return boundary + update


def shards(permeability):
    depth_total = ELZ * EZ
    shaped = permeability.reshape(
        3, permeability.shape[1], permeability.shape[2] // depth_total, depth_total
    )
    rimmed = padded_2(shaped, (("gx", 1), ("gy", 2)), MX)
    half_edge = EL // 2
    columns = shaped.shape[2] // EL

    def column_work(offset):
        block = lax.dynamic_slice_in_dim(rimmed, offset, EL + 2 * MX, 2)
        fine_block = jnp.pad(block, ((0, 0), (0, 0), (0, 0), (MZ, MZ)), mode="edge")
        twin_block = coarsen(fine_block)
        fine_local, fine_stiff = solve_column(fine_block, EL, ELZ, MX, MZ, 1.0)
        twin_local, twin_stiff = solve_column(
            twin_block, half_edge, ELZ // 2, MX // 2, MZ // 2, 2.0
        )
        return (fine_local, fine_stiff, twin_local, twin_stiff)

    offsets = jnp.arange(columns, dtype=jnp.int32) * EL
    fine_local, fine_stiff, twin_local, twin_stiff = lax.map(column_work, offsets)
    stiffness = jnp.stack([fine_stiff, twin_stiff])
    count = stiffness.shape[2]
    corner_first = spread_solve(stiffness, columns, count)
    corner_rows, corner_cols, corner_both = neighbours(corner_first)
    weights = corner_stack(corner_first, corner_rows, corner_cols, corner_both, count)
    fine_tiles = [
        pressure_tile(fine_local[column], weights[0, column], EL) for column in range(columns)
    ]
    twin_tiles = [
        pressure_tile(twin_local[column], weights[1, column], half_edge)
        for column in range(columns)
    ]
    fine_pressure = jnp.concatenate(fine_tiles, axis=1)
    twin_pressure = jnp.concatenate(twin_tiles, axis=1)
    return (fine_pressure.reshape(EL, -1), twin_pressure.reshape(half_edge, -1))


def solution(mesh):
    placed = (P(None, "gx", "gy"),)
    return jax.shard_map(
        shards,
        mesh=mesh,
        in_specs=placed,
        out_specs=(P("gx", "gy"), P("gx", "gy")),
        check_vma=False,
    )
```

profile of v0, /device:TPU:1, one launch (start us, length us, event | category | flops | bytes accessed | tf_op | source)
XLA Modules:
  0.0 635.2 jit_solution(149568154038995864)
XLA Ops:
  6.1 3.9 collective-permute-start.1
  13.8 4.4 collective-permute-done.4
  39.7 4.5 pad_maximum_fusion.3
  44.2 299.3 %while.21 = (s32[]{:T(128)}, f32[2,8,2,16,1024]{4,1,3,2,0:T(8,128)}, f32[2,2,8,8]{3,2,1,0:T(8,128)}, f32[2,8,2,8,256]{4,1,3,2,0:T(8,128)}, f32[2,2,8,8]{3,2,1,0:...) while((s32[]{:T(128)}, ...), condition=%wide.region_14.15_spmd, body=%wide.region_0.14_spmd.sunk | while | flops 130577320 | bytes 255059728 | solution.py:275
  90.3 5.9 reshape.1503
  96.2 5.7 slice.2293
  102.0 3.7 broadcast_in_dim.249
  106.8 3.9 reshape.1504
  131.4 26.2 %reshape.1505 = f32[3,20,2,20,2,18,2]{4,3,2,1,6,5,0:T(8,128)} reshape(f32[3,40,40,36]{2,1,3,0:T(8,128)} %pad_maximum_fusion.26) | data formatting | bytes 1382400 | tf_op jit(solution)/shard_map/while/body/eval_jaxpr/reshape | solution.py:170
  157.7 19.5 %reduce_sum.329 = f32[3,20,20,18]{2,1,3,0:T(8,128)S(1)} reduce(f32[3,20,2,20,2,18,2]{4,3,2,1,6,5,0:T(8,128)} %reshape.1505, f32[]{:T(128)} %constant.340.clone.31..sunk), dimensions={2,4,6}, to_apply=%region_7.7 | reduce | flops 151200 | bytes 777604 | tf_op jit(solution)/shard_map/while/body/eval_jaxpr/reduce_sum | solution.py:171
  235.5 5.9 reshape.1503
  241.5 5.7 slice.2293
  247.2 3.7 broadcast_in_dim.249
  252.0 4.0 reshape.1504
  271.7 3.0 fusion.264
  276.7 26.2 %reshape.1505 = f32[3,20,2,20,2,18,2]{4,3,2,1,6,5,0:T(8,128)} reshape(f32[3,40,40,36]{2,1,3,0:T(8,128)} %pad_maximum_fusion.26) | data formatting | bytes 1382400 | tf_op jit(solution)/shard_map/while/body/eval_jaxpr/reshape | solution.py:170
  302.9 19.7 %reduce_sum.329 = f32[3,20,20,18]{2,1,3,0:T(8,128)S(1)} reduce(f32[3,20,2,20,2,18,2]{4,3,2,1,6,5,0:T(8,128)} %reshape.1505, f32[]{:T(128)} %constant.340.clone.31..sunk), dimensions={2,4,6}, to_apply=%region_7.7 | reduce | flops 151200 | bytes 777604 | tf_op jit(solution)/shard_map/while/body/eval_jaxpr/reduce_sum | solution.py:171
  344.9 7.2 %collective-permute-done.6 = f32[2,2,3]{2,1,0:T(2,128)S(1)} collective-permute-done((f32[2,2,3]{2,1,0:T(2,128)S(1)}, f32[2,2,3]{2,1,0:T(2,128)S(1)}, u32[]{:S(2)}, u32[]{:S(2)}) %collective-permute-start.6) | collective-permute-done | bytes 80 | tf_op jit(solution)/shard_map/ppermute | solution.py:17
  352.2 4.6 collective-permute-done.7
  360.1 7.4 %collective-permute-start.9 = (f32[2,2,3]{2,1,0:T(2,128)S(1)}, f32[2,2,3]{2,1,0:T(2,128)S(1)}, u32[]{:S(2)}, u32[]{:S(2)}) collective-permute-start(f32[2,2,3]{2,1,0:T(2,128)S(1)} %pad_maximum_fusion.20), channel_id=1, source_target_pairs={{0,31},{1,0},{2,1},{3,2},{4,3},{5,4},{6,5},{7,6},{8,7},{9,8},{10,9... | collective-permute-start | bytes 152 | tf_op jit(solution)/shard_map/ppermute | solution.py:17
  371.6 4.2 collective-permute-done.11
  376.6 77.9 %all-reduce.72 = (f32[2,1,1]{0,2,1:T(1,128)S(1)}, f32[2,1,1]{0,2,1:T(1,128)S(1)}) all-reduce(f32[2,1,1]{0,2,1:T(1,128)S(1)} %bitcast.449, f32[2,1,1]{0,2,1:T(1,128)S(1)} %bitcast.448), channel_id=1, replica_groups=mesh['gx'=8,'gy'=32] {'gx','gy'}, use_global_device_ids=true, to_apply=%region_16.17 | all-reduce | flops 4 | bytes 32 | tf_op jit(solution)/shard_map/psum | solution.py:230
  454.7 73.6 %psum.30 = f32[2,1,1]{0,2,1:T(1,128)S(1)} all-reduce(f32[2,1,1]{0,2,1:T(1,128)S(1)} %bitcast.451), channel_id=1, replica_groups=mesh['gx'=8,'gy'=32] {'gx','gy'}, use_global_device_ids=true, to_apply=%region_20.21 | all-reduce | flops 2 | bytes 16 | tf_op jit(solution)/shard_map/psum | solution.py:230
  543.3 77.1 %psum.31 = f32[2,1,1]{0,2,1:T(1,128)S(1)} all-reduce(f32[2,1,1]{0,2,1:T(1,128)S(1)} %bitcast.450), channel_id=1, replica_groups=mesh['gx'=8,'gy'=32] {'gx','gy'}, use_global_device_ids=true, to_apply=%region_22.23 | all-reduce | flops 2 | bytes 16 | tf_op jit(solution)/shard_map/psum | solution.py:244
  (559 shorter events, 220.7 us)
Async XLA Ops:
  3.7 20.6 %collective-permute-start = (f32[3,4,64,32]{3,2,1,0:T(8,128)}, f32[3,4,64,32]{3,2,1,0:T(8,128)}, u32[]{:S(2)}, u32[]{:S(2)}) collective-permute-start(f32[3,4,64,32]{3,2,1,0:T(8,128)} %get-tuple-element.370), channel_id=1, source_target_pairs={{0,32},{32,64},{64,96},{96,128},{128,160},{160,192},{192,224},{224... | collective-permute-start | bytes 294920 | tf_op jit(solution)/shard_map/ppermute | solution.py:27
  6.1 19.5 %collective-permute-start.1 = (f32[3,4,64,32]{3,2,1,0:T(8,128)}, f32[3,4,64,32]{3,2,1,0:T(8,128)S(1)}, u32[]{:S(2)}, u32[]{:S(2)}) collective-permute-start(f32[3,4,64,32]{3,2,1,0:T(8,128)} %get-tuple-element.369), channel_id=1, source_target_pairs={{32,0},{64,32},{96,64},{128,96},{160,128},{192,160},{224,192},{0,2... | collective-permute-start | bytes 294920 | tf_op jit(solution)/shard_map/ppermute | solution.py:29
  10.1 20.1 %copy-start.18 = (f32[3]{0:T(128)}, f32[3]{0:T(128)S(1)}, u32[]{:S(2)}) copy-start(f32[3]{0:T(128)S(1)} %compare_convert_fusion) | copy-start | bytes 40
  10.1 8.1 %collective-permute-start.4 = (f32[2,2,3]{2,0,1:T(2,128)S(1)}, f32[2,2,3]{2,0,1:T(2,128)S(1)}, u32[]{:S(2)}, u32[]{:S(2)}) collective-permute-start(f32[2,2,3]{2,0,1:T(2,128)S(1)} %broadcast_in_dim.227), channel_id=1, source_target_pairs={{0,224},{32,0},{64,32},{96,64},{128,96},{160,128},{192,160},{224,1... | collective-permute-start | bytes 152 | tf_op jit(solution)/shard_map/ppermute | solution.py:17
  19.3 4.3 collective-permute-start.5
  25.4 4.9 copy-start.19
  27.6 7.9 %collective-permute-start.3 = (f32[3,40,4,32]{3,2,1,0:T(4,128)S(1)}, f32[3,40,4,32]{3,2,1,0:T(4,128)S(1)}, u32[]{:S(2)}, u32[]{:S(2)}) collective-permute-start(f32[3,40,4,32]{3,2,1,0:T(4,128)S(1)} %get-tuple-element.368), channel_id=1, source_target_pairs={{1,0},{2,1},{3,2},{4,3},{5,4},{6,5},{7,6},{8,7},{9,8},{10,9},{11,1... | collective-permute-start | bytes 184328 | tf_op jit(solution)/shard_map/ppermute | solution.py:29
  30.2 7.4 %collective-permute-start.2 = (f32[3,40,4,32]{3,2,1,0:T(4,128)S(1)}, f32[3,40,4,32]{3,2,1,0:T(4,128)S(1)}, u32[]{:S(2)}, u32[]{:S(2)}) collective-permute-start(f32[3,40,4,32]{3,2,1,0:T(4,128)S(1)} %get-tuple-element.367), channel_id=1, source_target_pairs={{0,1},{1,2},{2,3},{3,4},{4,5},{5,6},{6,7},{7,8},{8,9},{9,10},{10,1... | collective-permute-start | bytes 184328 | tf_op jit(solution)/shard_map/ppermute | solution.py:27
  125.3 4.6 copy-start.9
  125.3 4.6 copy-start.11
  270.5 4.6 copy-start.9
  270.5 4.6 copy-start.11
  344.8 7.3 %collective-permute-start.6 = (f32[2,2,3]{2,1,0:T(2,128)S(1)}, f32[2,2,3]{2,1,0:T(2,128)S(1)}, u32[]{:S(2)}, u32[]{:S(2)}) collective-permute-start(f32[2,2,3]{2,1,0:T(2,128)S(1)} %pad_maximum_fusion.19), channel_id=1, source_target_pairs={{0,1},{1,2},{2,3},{3,4},{4,5},{5,6},{6,7},{7,8},{8,9},{9,10},{10,1... | collective-permute-start | bytes 152 | tf_op jit(solution)/shard_map/ppermute | solution.py:17
  352.2 4.6 collective-permute-start.7
  357.6 2.4 collective-permute-start.8
  360.1 8.2 %collective-permute-start.9 = (f32[2,2,3]{2,1,0:T(2,128)S(1)}, f32[2,2,3]{2,1,0:T(2,128)S(1)}, u32[]{:S(2)}, u32[]{:S(2)}) collective-permute-start(f32[2,2,3]{2,1,0:T(2,128)S(1)} %pad_maximum_fusion.20), channel_id=1, source_target_pairs={{0,31},{1,0},{2,1},{3,2},{4,3},{5,4},{6,5},{7,6},{8,7},{9,8},{10,9... | collective-permute-start | bytes 152 | tf_op jit(solution)/shard_map/ppermute | solution.py:17
  370.2 1.2 collective-permute-start.10
  371.5 4.2 collective-permute-start.11
  528.5 2.7 collective-permute-start.12
  531.2 3.9 collective-permute-start.13
  537.0 1.2 collective-permute-start.14
  538.3 4.2 collective-permute-start.15
  621.2 2.7 collective-permute-start.16
  623.9 3.7 collective-permute-start.17
  (33 other events, 62.1 us)
where the time goes:
time: 646 us; the launch traced here: 635 us
  blocking collectives  229 us (35%)
  local copies, waits for them, and re-layouts  188 us (29%)
  other arithmetic  118 us (18%)
  waiting for transfers between devices  34.7 us (5%)
  starting transfers between devices  28.8 us (4%)
  matrix products  20.8 us (3%)
  loops' own time  14.6 us (2%)
    psum x2, blocking collectives, squares(): lax.psum(jnp.sum(residual * residual, axis=(1, 2), keepdims=True), ('gx',...  152 us
    psum x1, blocking collectives, spread_solve(): lax.psum(jnp.sum(direction * image, axis=(1, 2), keepdims=True), ('gx', '...  77.1 us
    reshape x2, local copies, waits for them, and re-layouts, coarsen(): grouped = block.reshape(comps, rows // 2, 2, width // 2, 2, depth // 2, 2)  52.5 us
    reduce_sum x2, other arithmetic, coarsen(): return 0.125 * jnp.sum(grouped, axis=(2, 4, 6))  39.3 us
    ppermute x14, waiting for transfers between devices, shifted(): lax.ppermute(shard, axis, [(i, (i + by) % count) for i in range(count)])  34.7 us
    ppermute x14, starting transfers between devices, shifted(): lax.ppermute(shard, axis, [(i, (i + by) % count) for i in range(count)])  19.8 us
    reshape x4, local copies, waits for them, and re-layouts, solve_column(): solution.reshape(8, count, depth, rows, width)  15.7 us
    slice x4, local copies, waits for them, and re-layouts, solve_column(): solution.reshape(8, count, depth, rows, width)  15 us
  transfers between devices with their start and end apart: 18, of which 14 were waited for; matrix products, arithmetic and copies ran while one was open for 2% of the time, Pallas kernels for 0%

commit v1 on v0

--- a/solution.py
+++ b/solution.py
@@ -242,7 +242,7 @@
     for step in range(COARSE_ITERS):
         image = inside * local_operator(stiffness, direction, count)
         alpha = norm_now / lax.psum(
-            jnp.sum(direction * image, axis=(1, 2), keepdims=True), ("gx", "gy")
+            lax.psum(jnp.sum(direction * image, axis=(1, 2), keepdims=True), "gy"), "gx"
         )
         update = update + alpha * direction
         residual = residual - alpha * image

time: 646 us -> 729 us (1.13)
  blocking collectives: 229 us -> 309 us
    psum x1 -> x4, blocking collectives: 77.1 us -> 160 us  [the longest x2 136 us: spread_solve(): lax.psum(jnp.sum(direction * image, axis=(1, 2), keepdims=True), 'gy')]
where the time goes in v1:
time: 729 us; the launch traced here: 718 us
  blocking collectives  309 us (42%)
  local copies, waits for them, and re-layouts  187 us (26%)
  other arithmetic  119 us (16%)
  waiting for transfers between devices  34.1 us (5%)
  starting transfers between devices  31.5 us (4%)
  matrix products  20.8 us (3%)
  loops' own time  14.7 us (2%)
    psum x2, blocking collectives, squares(): lax.psum(jnp.sum(residual * residual, axis=(1, 2), keepdims=True), ('gx',...  150 us
    psum x2, blocking collectives, spread_solve(): lax.psum(jnp.sum(direction * image, axis=(1, 2), keepdims=True), 'gy')  136 us
    reshape x2, local copies, waits for them, and re-layouts, coarsen(): grouped = block.reshape(comps, rows // 2, 2, width // 2, 2, depth // 2, 2)  52.3 us
    reduce_sum x2, other arithmetic, coarsen(): return 0.125 * jnp.sum(grouped, axis=(2, 4, 6))  39.3 us
    ppermute x14, waiting for transfers between devices, shifted(): lax.ppermute(shard, axis, [(i, (i + by) % count) for i in range(count)])  34.1 us
    psum x2, blocking collectives, spread_solve(): lax.psum(lax.psum(jnp.sum(direction * image, axis=(1, 2), keepdims=True),...  23.9 us
    ppermute x14, starting transfers between devices, shifted(): lax.ppermute(shard, axis, [(i, (i + by) % count) for i in range(count)])  22.5 us
    reshape x4, local copies, waits for them, and re-layouts, solve_column(): solution.reshape(8, count, depth, rows, width)  15.6 us
  transfers between devices with their start and end apart: 18, of which 14 were waited for; matrix products, arithmetic and copies ran while one was open for 2% of the time, Pallas kernels for 0%

profile of v1, /device:TPU:1, one launch (start us, length us, event | category | flops | bytes accessed | tf_op | source)
XLA Modules:
  0.0 717.8 jit_solution(9210242526984584936)
XLA Ops:
  6.1 3.9 collective-permute-start.1
  13.8 4.4 collective-permute-done.4
  39.8 4.5 pad_maximum_fusion.3
  44.3 299.0 %while.21 = (s32[]{:T(128)}, f32[2,8,2,16,1024]{4,1,3,2,0:T(8,128)}, f32[2,2,8,8]{3,2,1,0:T(8,128)}, f32[2,8,2,8,256]{4,1,3,2,0:T(8,128)}, f32[2,2,8,8]{3,2,1,0:...) while((s32[]{:T(128)}, ...), condition=%wide.region_14.15_spmd, body=%wide.region_0.14_spmd.sunk | while | flops 130577320 | bytes 255059728 | solution.py:275
  90.3 5.9 reshape.1503
  96.2 5.7 slice.2293
  131.4 26.2 %reshape.1505 = f32[3,20,2,20,2,18,2]{4,3,2,1,6,5,0:T(8,128)} reshape(f32[3,40,40,36]{2,1,3,0:T(8,128)} %pad_maximum_fusion.26) | data formatting | bytes 1382400 | tf_op jit(solution)/shard_map/while/body/eval_jaxpr/reshape | solution.py:170
  157.6 19.5 %reduce_sum.329 = f32[3,20,20,18]{2,1,3,0:T(8,128)S(1)} reduce(f32[3,20,2,20,2,18,2]{4,3,2,1,6,5,0:T(8,128)} %reshape.1505, f32[]{:T(128)} %constant.340.clone.31..sunk), dimensions={2,4,6}, to_apply=%region_7.7 | reduce | flops 151200 | bytes 777604 | tf_op jit(solution)/shard_map/while/body/eval_jaxpr/reduce_sum | solution.py:171
  235.4 5.9 reshape.1503
  241.3 5.7 slice.2293
  251.8 4.0 reshape.1504
  276.5 26.2 %reshape.1505 = f32[3,20,2,20,2,18,2]{4,3,2,1,6,5,0:T(8,128)} reshape(f32[3,40,40,36]{2,1,3,0:T(8,128)} %pad_maximum_fusion.26) | data formatting | bytes 1382400 | tf_op jit(solution)/shard_map/while/body/eval_jaxpr/reshape | solution.py:170
  302.7 19.7 %reduce_sum.329 = f32[3,20,20,18]{2,1,3,0:T(8,128)S(1)} reduce(f32[3,20,2,20,2,18,2]{4,3,2,1,6,5,0:T(8,128)} %reshape.1505, f32[]{:T(128)} %constant.340.clone.31..sunk), dimensions={2,4,6}, to_apply=%region_7.7 | reduce | flops 151200 | bytes 777604 | tf_op jit(solution)/shard_map/while/body/eval_jaxpr/reduce_sum | solution.py:171
  344.6 7.2 %collective-permute-done.6 = f32[2,2,3]{2,1,0:T(2,128)S(1)} collective-permute-done((f32[2,2,3]{2,1,0:T(2,128)S(1)}, f32[2,2,3]{2,1,0:T(2,128)S(1)}, u32[]{:S(2)}, u32[]{:S(2)}) %collective-permute-start.6) | collective-permute-done | bytes 80 | tf_op jit(solution)/shard_map/ppermute | solution.py:17
  351.9 4.6 collective-permute-done.7
  359.8 7.4 %collective-permute-start.9 = (f32[2,2,3]{2,1,0:T(2,128)S(1)}, f32[2,2,3]{2,1,0:T(2,128)S(1)}, u32[]{:S(2)}, u32[]{:S(2)}) collective-permute-start(f32[2,2,3]{2,1,0:T(2,128)S(1)} %pad_maximum_fusion.20), channel_id=1, source_target_pairs={{0,31},{1,0},{2,1},{3,2},{4,3},{5,4},{6,5},{7,6},{8,7},{9,8},{10,9... | collective-permute-start | bytes 152 | tf_op jit(solution)/shard_map/ppermute | solution.py:17
  371.2 4.2 collective-permute-done.11
  376.3 68.3 %psum.43 = f32[2,1,1]{0,2,1:T(1,128)S(1)} all-reduce(f32[2,1,1]{0,2,1:T(1,128)S(1)} %bitcast.449), channel_id=1, replica_groups=mesh['gx'=8,'gy'=32] {'gy'}, use_global_device_ids=true, to_apply=%region_18.19 | all-reduce | flops 2 | bytes 16 | tf_op jit(solution)/shard_map/psum | solution.py:245
  444.6 73.9 %psum.42 = f32[2,1,1]{0,2,1:T(1,128)S(1)} all-reduce(f32[2,1,1]{0,2,1:T(1,128)S(1)} %bitcast.448), channel_id=1, replica_groups=mesh['gx'=8,'gy'=32] {'gx','gy'}, use_global_device_ids=true, to_apply=%region_16.17 | all-reduce | flops 2 | bytes 16 | tf_op jit(solution)/shard_map/psum | solution.py:230
  518.5 11.6 %psum.44 = f32[2,1,1]{0,2,1:T(1,128)S(1)} all-reduce(f32[2,1,1]{0,2,1:T(1,128)S(1)} %psum.43), channel_id=1, replica_groups=mesh['gx'=8,'gy'=32] {'gx'}, use_global_device_ids=true, to_apply=%region_19.20 | all-reduce | flops 2 | bytes 16 | tf_op jit(solution)/shard_map/psum | solution.py:244
  530.2 75.7 %psum.45 = f32[2,1,1]{0,2,1:T(1,128)S(1)} all-reduce(f32[2,1,1]{0,2,1:T(1,128)S(1)} %bitcast.451), channel_id=1, replica_groups=mesh['gx'=8,'gy'=32] {'gx','gy'}, use_global_device_ids=true, to_apply=%region_21.22 | all-reduce | flops 2 | bytes 16 | tf_op jit(solution)/shard_map/psum | solution.py:230
  620.3 67.6 %psum.46 = f32[2,1,1]{0,2,1:T(1,128)S(1)} all-reduce(f32[2,1,1]{0,2,1:T(1,128)S(1)} %bitcast.450), channel_id=1, replica_groups=mesh['gx'=8,'gy'=32] {'gy'}, use_global_device_ids=true, to_apply=%region_23.24 | all-reduce | flops 2 | bytes 16 | tf_op jit(solution)/shard_map/psum | solution.py:245
  687.9 12.3 %psum.47 = f32[2,1,1]{0,2,1:T(1,128)S(1)} all-reduce(f32[2,1,1]{0,2,1:T(1,128)S(1)} %psum.46), channel_id=1, replica_groups=mesh['gx'=8,'gy'=32] {'gx'}, use_global_device_ids=true, to_apply=%region_24.25 | all-reduce | flops 2 | bytes 16 | tf_op jit(solution)/shard_map/psum | solution.py:244
  703.8 5.5 collective-permute-start.17
  (562 shorter events, 231.6 us)
Async XLA Ops:
  3.7 20.6 %collective-permute-start = (f32[3,4,64,32]{3,2,1,0:T(8,128)}, f32[3,4,64,32]{3,2,1,0:T(8,128)}, u32[]{:S(2)}, u32[]{:S(2)}) collective-permute-start(f32[3,4,64,32]{3,2,1,0:T(8,128)} %get-tuple-element.368), channel_id=1, source_target_pairs={{0,32},{32,64},{64,96},{96,128},{128,160},{160,192},{192,224},{224... | collective-permute-start | bytes 294920 | tf_op jit(solution)/shard_map/ppermute | solution.py:27
  6.1 19.4 %collective-permute-start.1 = (f32[3,4,64,32]{3,2,1,0:T(8,128)}, f32[3,4,64,32]{3,2,1,0:T(8,128)S(1)}, u32[]{:S(2)}, u32[]{:S(2)}) collective-permute-start(f32[3,4,64,32]{3,2,1,0:T(8,128)} %get-tuple-element.367), channel_id=1, source_target_pairs={{32,0},{64,32},{96,64},{128,96},{160,128},{192,160},{224,192},{0,2... | collective-permute-start | bytes 294920 | tf_op jit(solution)/shard_map/ppermute | solution.py:29
  10.1 20.1 %copy-start.18 = (f32[3]{0:T(128)}, f32[3]{0:T(128)S(1)}, u32[]{:S(2)}) copy-start(f32[3]{0:T(128)S(1)} %compare_convert_fusion) | copy-start | bytes 40
  10.1 8.1 %collective-permute-start.4 = (f32[2,2,3]{2,0,1:T(2,128)S(1)}, f32[2,2,3]{2,0,1:T(2,128)S(1)}, u32[]{:S(2)}, u32[]{:S(2)}) collective-permute-start(f32[2,2,3]{2,0,1:T(2,128)S(1)} %broadcast_in_dim.227), channel_id=1, source_target_pairs={{0,224},{32,0},{64,32},{96,64},{128,96},{160,128},{192,160},{224,1... | collective-permute-start | bytes 152 | tf_op jit(solution)/shard_map/ppermute | solution.py:17
  19.3 4.3 collective-permute-start.5
  25.3 4.9 copy-start.19
  27.6 8.0 %collective-permute-start.3 = (f32[3,40,4,32]{3,2,1,0:T(4,128)S(1)}, f32[3,40,4,32]{3,2,1,0:T(4,128)S(1)}, u32[]{:S(2)}, u32[]{:S(2)}) collective-permute-start(f32[3,40,4,32]{3,2,1,0:T(4,128)S(1)} %get-tuple-element.366), channel_id=1, source_target_pairs={{1,0},{2,1},{3,2},{4,3},{5,4},{6,5},{7,6},{8,7},{9,8},{10,9},{11,1... | collective-permute-start | bytes 184328 | tf_op jit(solution)/shard_map/ppermute | solution.py:29
  30.2 7.5 %collective-permute-start.2 = (f32[3,40,4,32]{3,2,1,0:T(4,128)S(1)}, f32[3,40,4,32]{3,2,1,0:T(4,128)S(1)}, u32[]{:S(2)}, u32[]{:S(2)}) collective-permute-start(f32[3,40,4,32]{3,2,1,0:T(4,128)S(1)} %get-tuple-element.365), channel_id=1, source_target_pairs={{0,1},{1,2},{2,3},{3,4},{4,5},{5,6},{6,7},{7,8},{8,9},{9,10},{10,1... | collective-permute-start | bytes 184328 | tf_op jit(solution)/shard_map/ppermute | solution.py:27
  125.2 4.6 copy-start.9
  125.2 4.6 copy-start.11
  270.3 4.6 copy-start.9
  270.3 4.6 copy-start.11
  344.6 7.3 %collective-permute-start.6 = (f32[2,2,3]{2,1,0:T(2,128)S(1)}, f32[2,2,3]{2,1,0:T(2,128)S(1)}, u32[]{:S(2)}, u32[]{:S(2)}) collective-permute-start(f32[2,2,3]{2,1,0:T(2,128)S(1)} %pad_maximum_fusion.19), channel_id=1, source_target_pairs={{0,1},{1,2},{2,3},{3,4},{4,5},{5,6},{6,7},{7,8},{8,9},{9,10},{10,1... | collective-permute-start | bytes 152 | tf_op jit(solution)/shard_map/ppermute | solution.py:17
  351.9 4.6 collective-permute-start.7
  357.3 2.4 collective-permute-start.8
  359.8 8.2 %collective-permute-start.9 = (f32[2,2,3]{2,1,0:T(2,128)S(1)}, f32[2,2,3]{2,1,0:T(2,128)S(1)}, u32[]{:S(2)}, u32[]{:S(2)}) collective-permute-start(f32[2,2,3]{2,1,0:T(2,128)S(1)} %pad_maximum_fusion.20), channel_id=1, source_target_pairs={{0,31},{1,0},{2,1},{3,2},{4,3},{5,4},{6,5},{7,6},{8,7},{9,8},{10,9... | collective-permute-start | bytes 152 | tf_op jit(solution)/shard_map/ppermute | solution.py:17
  369.9 1.2 collective-permute-start.10
  371.2 4.2 collective-permute-start.11
  606.1 2.8 collective-permute-start.12
  608.9 3.1 collective-permute-start.13
  614.0 1.2 collective-permute-start.14
  615.2 4.2 collective-permute-start.15
  701.1 2.7 collective-permute-start.16
  703.8 6.3 collective-permute-start.17
  (33 other events, 62.0 us)
